TPU v7x, 768 devices: a whole 4x8x12 slice. The times are simulated.
768 devices in a mesh: wave: 48 (over y, z_hi, core), atom: 16 (over x, z_lo).
Axes of the slice: x: 4, y: 8, z: 12 (z_hi: 3, z_lo: 4; z = z_hi * 4 + z_lo), core: 2. Of those that a mesh axis runs over, the one named last changes fastest.
Arguments:
- slab: float32 [24576, 2048], P('wave', 'atom'), may hold values from -0.0390625 to 0.0390625
- orbitals: float32 [24576, 256], P('wave'), may hold values from -6 to 6
- sphere_ops: float32 [3, 32, 64, 64], P(None, 'atom'), may hold values from -0.75 to 0.75
- wave_terms: float32 [3, 24576], P(None, 'wave'), may hold values from -1 to 1
Outputs:
- applied: float32 [3, 24576, 256], P(None, ('wave', 'atom'))
All inputs are finite; a program needn't handle non-finite values.
Results may differ from a plain program's by a relative error of at most 0.0001.
Values sent between devices are 32-bit elements; how exact they have to be, the bound alone decides.
No kernel may reach another device: no remote copies, remote signals or barrier semaphores. Data moves between devices by JAX's collectives and lax.ppermute only.
A program may use at most 32 MiB of HBM per device.

v0:
```python
import jax
import jax.numpy as jnp
from jax import lax
from jax.sharding import PartitionSpec as P


def shards(slab, orbitals, sphere_ops, wave_terms):
    partial_value = jnp.dot(
        slab.T, orbitals, preferred_element_type=jnp.float32, precision=lax.Precision.HIGHEST
    )
    coeffs = lax.psum(partial_value, "wave")
    atoms_here = sphere_ops.shape[1]
    width = sphere_ops.shape[2]
    blocks = coeffs.reshape(atoms_here, width, coeffs.shape[1])
    inner = jnp.einsum("dalm,amb->dalb", sphere_ops, blocks, precision=lax.Precision.HIGHEST)
    inner = inner.reshape(3, atoms_here * width, coeffs.shape[1])
    own_rows = orbitals.shape[0] // lax.axis_size("atom")
    first_row = lax.axis_index("atom") * own_rows
    own_orbitals = lax.dynamic_slice_in_dim(orbitals, first_row, own_rows, 0)
    own_factors = lax.dynamic_slice_in_dim(wave_terms, first_row, own_rows, 1)
    local_part = own_factors[:, :, None] * own_orbitals[None]
    terms = jnp.einsum("ws,dsb->dwb", slab, inner, precision=lax.Precision.HIGHEST)
    summed = lax.psum_scatter(terms, "atom", scatter_dimension=1, tiled=True)
    return summed + local_part


def solution(mesh):
    return jax.shard_map(
        shards,
        mesh=mesh,
        in_specs=(P("wave", "atom"), P("wave", None), P(None, "atom", None, None), P(None, "wave")),
        out_specs=P(None, ("wave", "atom"), None),
        check_vma=False,
    )
```

profile of v0, /device:TPU:32, one launch (start us, length us, event | category | flops | bytes accessed | tf_op | source)
XLA Modules:
  0.0 681.1 jit_solution(10878799437352348980)
XLA Ops:
  6.5 0.0 copy-start
  6.5 0.0 copy-start.1
  6.5 0.0 all-reduce.4.cloned.1.call-start
  6.5 1.0 copy-done
  7.6 2.2 fusion.3
  9.8 0.0 all-reduce.4.cloned.1.call-update
  9.8 0.0 all-reduce.6.cloned.1.call-start
  9.9 471.7 %all-reduce.4.cloned.1.call-done = f32[2,64,256]{2,1,0:T(8,128)} async-done(((f32[2,64,256]{2,1,0:T(8,128)}), f32[2,64,256]{2,1,0:T(8,128)}) %all-reduce.4.cloned.1.call-update) | async-done | bytes 131088 | tf_op jit(solution)/shard_map/psum | solution.py:11
  481.5 1.4 convolution_bitcast_fusion.1
  483.0 0.0 copy-done.1
  483.0 1.4 convolution_bitcast_fusion
  484.5 1.8 copy.16
  486.3 0.0 all-reduce.6.cloned.1.call-update
  486.3 0.8 constant_dynamic-slice_fusion.1
  487.1 0.1 copy.17
  487.1 1.3 dynamic-slice
  489.1 183.5 %all-reduce.6.cloned.1.call-done = f32[3,512,256]{2,0,1:T(4,128)} async-done(((f32[3,512,256]{2,0,1:T(4,128)}), f32[3,512,256]{2,0,1:T(4,128)}) %all-reduce.6.cloned.1.call-update) | async-done | bytes 1572880
  672.6 1.0 dynamic-slice_add_fusion
  673.6 0.7 copy.18
  (2 shorter events, 0.0 us)
Async XLA Ops:
  6.5 1.0 copy-start
  6.5 476.5 %copy-start.1 = (f32[512,128]{1,0:T(8,128)S(1)}, f32[512,128]{1,0:T(8,128)}, u32[]{:S(2)}) copy-start(f32[512,128]{1,0:T(8,128)} %param.4) | copy-start | bytes 786436
  6.5 475.0 %all-reduce.4.cloned.1.call-start = ((), (), s32[]{:S(2)}) async-start(), calls=%async_computation | async-start | bytes 262144 | tf_op jit(solution)/shard_map/psum | solution.py:11
  9.8 662.8 %all-reduce.6.cloned.1.call-start = ((), (), s32[]{:S(2)}) async-start(), calls=%async_computation.1 | async-start | bytes 4194304
Sparse Core Ops, SparseCore 0:
  10.5 470.9 all-reduce.3
  486.4 186.1 all-reduce.5
where the time goes:
time: 682 us; the launch traced here: 681 us
  waiting for transfers between devices  655 us (96%)
  between operations  14.1 us (2%)
    psum x1, waiting for transfers between devices, shards(): coeffs = lax.psum(partial_value, 'wave')  472 us
    unnamed x3, waiting for transfers between devices  184 us
  transfers between devices with their start and end apart: 2, of which 2 were waited for; matrix products, arithmetic and copies ran while one was open for 0% of the time, Pallas kernels for 0%

commit v1 on v0

v1 whole, which is shorter than its diff:
```python
import jax
import jax.numpy as jnp
from jax import lax
from jax.experimental import pallas as pl
from jax.experimental.pallas import tpu as pltpu
from jax.sharding import Mesh, PartitionSpec as P


GATHER, REDUCE = "zl", "x"
THIRD, FOURTH = ("zh",), ("y", GATHER)
VMEM = pl.BlockSpec(memory_space=pltpu.VMEM)


def exchange(blocks, axes):
    return lax.all_to_all(blocks, axes, 0, 0, tiled=True)


def gather(block, axes):
    n = lax.axis_size(axes)
    return exchange(jnp.broadcast_to(block[None], (n,) + block.shape), axes)


def swap(block, axis, bit):
    n = lax.axis_size(axis)
    return lax.ppermute(block, axis, [(i, i ^ bit) for i in range(n)])


def split(a):
    high = a.astype(jnp.bfloat16)
    return high, (a - high.astype(jnp.float32)).astype(jnp.bfloat16)


def dot3(a, b, dims=(((1,), (0,)), ((), ()))):
    (ah, al), (bh, bl) = a, b
    f = lambda u, v: lax.dot_general(u, v, dims, preferred_element_type=jnp.float32)
    return f(ah, bh) + (f(ah, bl) + f(al, bh))


def first_kernel(slab_ref, orb_ref, out_ref):
    n, sub, half = out_ref.shape
    nc = orb_ref.shape[1] // half
    part = dot3(split(slab_ref[...].T), split(orb_ref[...]))
    for y in range(n // nc):
        for c in range(nc):
            out_ref[y * nc + c] = part[y * sub : (y + 1) * sub, c * half : (c + 1) * half]


def apply(slab, orbitals, sphere_ops, wave_terms):
    ny, nzh, nc, nx, nzl = (lax.axis_size(n) for n in ("y", "zh", "c", "x", "zl"))
    ng, nr = lax.axis_size(GATHER), lax.axis_size(REDUCE)
    rows, width = slab.shape
    nb = orbitals.shape[1]
    half = nb // nc
    own_rows = rows // (nx * nzl)
    nd, atoms, lm = sphere_ops.shape[:3]
    sub = width // ny
    me, core = lax.axis_index(GATHER), lax.axis_index("c")
    f32 = lambda *s: jax.ShapeDtypeStruct(s, jnp.float32)

    part = pl.pallas_call(
        first_kernel, out_shape=f32(ny * nc, sub, half), in_specs=[VMEM] * 2, out_specs=VMEM, name="first_dot"
    )(slab, orbitals)
    mine = exchange(part, ("y", "c"))

    n_slab, n_ops = nr * own_rows, nd * lm // nc
    rowset = slab.reshape(nx, nzl, own_rows, width)
    pick = lambda j: lax.dynamic_index_in_dim(
        rowset, jnp.bitwise_xor(me, j), 1 if GATHER == "zl" else 0, keepdims=False
    ).reshape(n_slab, width)
    ops = lax.dynamic_index_in_dim(sphere_ops.reshape(nc, n_ops, width), core, 0, keepdims=False)
    near = jnp.concatenate([pick(1), ops, pick(3)], axis=0)
    own = jnp.concatenate([pick(0), ops], axis=0)
    to_far = pick(2)
    got_near = swap(near, GATHER, 1)
    far = jnp.concatenate([to_far, ops, got_near[n_slab + n_ops :], got_near[n_slab : n_slab + n_ops]], axis=0)
    got_far = swap(far, GATHER, 2)
    n_all = n_slab + n_ops
    stacked = jnp.stack([own, got_near[:n_all], got_far[:n_all], got_far[n_all:]])
    other = swap(stacked, "c", 1)
    both = [jnp.where(core == c, stacked, other) for c in range(nc)]
    got = jnp.stack(both, axis=1)
    odd, high = jnp.bitwise_and(me, 1) == 1, me >= 2
    pairs = [jnp.where(odd, got[j ^ 1], got[j]) for j in range(4)]
    got = jnp.stack([jnp.where(high, pairs[j ^ 2], pairs[j]) for j in range(4)])
    slab_g = got[:, :, :n_slab]
    ops_g = got[:, :, n_slab:].reshape(ng, nd, atoms, lm, lm)

    first_row = (lax.axis_index("x") * nzl + lax.axis_index("zl")) * own_rows
    own_orbitals = lax.dynamic_slice_in_dim(orbitals, first_row, own_rows, 0)
    own_factors = lax.dynamic_slice_in_dim(wave_terms, first_row, own_rows, 1)
    local = own_factors[:, :, None] * own_orbitals[None]

    mine = mine.sum(0)
    mine = gather(mine, THIRD).reshape((nzh, -1, sub, half))
    mine = mine.sum(0)
    coeffs = gather(mine, FOURTH).reshape(ny, ng, sub, half)
    coeffs = coeffs.transpose(1, 0, 2, 3).reshape(ng, atoms, lm, half)
    inner = jnp.einsum("gdalm,gamb->dgalb", ops_g, coeffs, precision=lax.Precision.HIGH)
    inner = inner.reshape(nd, ng, width, half)
    terms = jnp.einsum("gcws,dgsb->cdwb", slab_g, inner, precision=lax.Precision.HIGH)
    terms = terms.reshape(nc, nd, nr, own_rows, half).transpose(0, 2, 1, 3, 4)
    summed = exchange(terms.reshape(nc * nr, nd, own_rows, half), ("c", REDUCE))
    summed = summed.reshape(nc, nr, nd, own_rows, half).sum(1)
    summed = summed.transpose(1, 2, 0, 3).reshape(nd, own_rows, nb)
    return summed + local


def solution(mesh):
    fine = Mesh(mesh.devices.reshape(8, 3, 2, 4, 4), ("y", "zh", "c", "x", "zl"))
    wave, atom = ("y", "zh", "c"), ("x", "zl")
    return jax.shard_map(
        apply,
        mesh=fine,
        in_specs=(P(wave, atom), P(wave, None), P(None, atom, None, None), P(None, wave)),
        out_specs=P(None, wave + atom, None),
        check_vma=False,
    )
```

time: 682 us -> 102 us (0.15)
  the two profiles are of different devices: /device:TPU:32 before, /device:TPU:1 now
where the time goes in v1:
time: 102 us; the launch traced here: 101 us
  starting transfers between devices  46.3 us (45%)
  waiting for transfers between devices  32.7 us (32%)
  blocking collectives  13.3 us (13%)
  local copies, waits for them, and re-layouts  4.4 us (4%)
  Pallas kernels  2.11 us (2%)
  other arithmetic  1.13 us (1%)
  matrix products  1.06 us (1%)
    all_to_all x3, waiting for transfers between devices, exchange(): return lax.all_to_all(blocks, axes, 0, 0, tiled=True)  24 us
    all_to_all x3, starting transfers between devices, exchange(): return lax.all_to_all(blocks, axes, 0, 0, tiled=True)  24 us
    ppermute x3, starting transfers between devices, swap(): return lax.ppermute(block, axis, [(i, i ^ bit) for i in range(n)])  22.3 us
    all_to_all x1, blocking collectives, exchange(): return lax.all_to_all(blocks, axes, 0, 0, tiled=True)  13.3 us
    ppermute x3, waiting for transfers between devices, swap(): return lax.ppermute(block, axis, [(i, i ^ bit) for i in range(n)])  8.69 us
    pallas_call x1, Pallas kernels, apply(): pl.pallas_call(first_kernel, out_shape=f32(ny * nc, sub, half), in_specs=...  2.11 us
  transfers between devices with their start and end apart: 6, of which 5 were waited for; matrix products, arithmetic and copies ran while one was open for 3% of the time, Pallas kernels for 2%

profile of v1, /device:TPU:1, one launch (start us, length us, event | category | flops | bytes accessed | tf_op | source)
XLA Modules:
  0.0 101.3 jit_solution(1362554774235024205)
XLA Ops:
  0.0 0.0 copy-start
  0.0 0.0 copy-start.1
  0.0 1.1 %reshape.57 = f32[2,96,128]{2,1,0:T(8,128)S(1)} reshape(f32[3,2,64,64]{3,2,1,0:T(8,128)} %param.6) | data formatting | bytes 196608 | tf_op jit(solution)/shard_map/reshape | solution.py:70
  1.1 0.0 copy-done.1
  1.2 4.8 %collective-permute-start = (f32[352,128]{1,0:T(8,128)S(1)}, f32[352,128]{1,0:T(8,128)S(1)}, u32[]{:S(2)}, u32[]{:S(2)}) collective-permute-start(f32[352,128]{1,0:T(8,128)S(1)} %pad_maximum_fusion.10), channel_id=1, source_target_pairs={{0,1},{1,0},{2,3},{3,2},{4,5},{5,4},{6,7},{7,6},{8,9},{9,8},{10,11... | collective-permute-start | bytes 540680 | tf_op jit(solution)/shard_map/ppermute | solution.py:25
  6.0 2.9 %collective-permute-done = f32[352,128]{1,0:T(8,128)S(1)} collective-permute-done((f32[352,128]{1,0:T(8,128)S(1)}, f32[352,128]{1,0:T(8,128)S(1)}, u32[]{:S(2)}, u32[]{:S(2)}) %collective-permute-start) | collective-permute-done | bytes 180256 | tf_op jit(solution)/shard_map/ppermute | solution.py:25
  8.9 7.2 %collective-permute-start.1 = (f32[448,128]{1,0:T(8,128)S(1)}, f32[448,128]{1,0:T(8,128)S(1)}, u32[]{:S(2)}, u32[]{:S(2)}) collective-permute-start(f32[448,128]{1,0:T(8,128)S(1)} %pad_maximum_fusion.9), channel_id=1, source_target_pairs={{0,2},{1,3},{2,0},{3,1},{4,6},{5,7},{6,4},{7,5},{8,10},{9,11},{10,... | collective-permute-start | bytes 688136 | tf_op jit(solution)/shard_map/ppermute | solution.py:25
  16.1 5.8 %collective-permute-done.1 = f32[448,128]{1,0:T(8,128)S(1)} collective-permute-done((f32[448,128]{1,0:T(8,128)S(1)}, f32[448,128]{1,0:T(8,128)S(1)}, u32[]{:S(2)}, u32[]{:S(2)}) %collective-permute-start.1) | collective-permute-done | bytes 229408 | tf_op jit(solution)/shard_map/ppermute | solution.py:25
  22.0 10.3 %collective-permute-start.2 = (f32[4,224,128]{2,1,0:T(8,128)S(1)}, f32[4,224,128]{2,1,0:T(8,128)S(1)}, u32[]{:S(2)}, u32[]{:S(2)}) collective-permute-start(f32[4,224,128]{2,1,0:T(8,128)S(1)} %pad_maximum_fusion.5), channel_id=1, source_target_pairs={{0,16},{16,0},{1,17},{17,1},{2,18},{18,2},{3,19},{19,3},{4,20},{20... | collective-permute-start | bytes 1376264 | tf_op jit(solution)/shard_map/ppermute | solution.py:25
  32.3 2.1 %first_dot.1 = f32[16,16,128]{2,1,0:T(8,128)} custom-call(f32[512,128]{1,0:T(8,128)} %slab_ref.1, f32[512,256]{1,0:T(8,128)} %orb_ref.1), custom_call_target="tpu_custom_call" | custom-call | tf_op jit(solution)/shard_map/first_dot/pallas_call | solution.py:60
  34.4 13.3 %all_to_all.20 = f32[16,16,128]{2,1,0:T(8,128)S(1)} all-to-all(f32[16,16,128]{2,1,0:T(8,128)} %first_dot.1), channel_id=1, replica_groups=mesh['y'=8,'zh'=3,'c'=2,'x'=4,'zl'=4] {'y','c'}, dimensions={0} | all-to-all | bytes 262144 | tf_op jit(solution)/shard_map/all_to_all | solution.py:15
  47.8 0.6 broadcast_in_dim.4
  48.4 11.2 %all-to-all-start.1 = ((f32[3,16,128]{2,1,0:T(8,128)}), f32[3,16,128]{2,1,0:T(8,128)S(1)}, u32[]{:S(2)}, u32[]{:S(2)}) async-start(f32[3,16,128]{2,1,0:T(8,128)} %broadcast_in_dim.4), calls=%async_computation.1 | async-start | bytes 49152 | tf_op jit(solution)/shard_map/all_to_all | solution.py:15
  59.6 6.6 %all-to-all-done.1 = f32[3,16,128]{2,1,0:T(8,128)S(1)} async-done(((f32[3,16,128]{2,1,0:T(8,128)}), f32[3,16,128]{2,1,0:T(8,128)S(1)}, u32[]{:S(2)}, u32[]{:S(2)}) %all-to-all-start.1) | async-done | bytes 24608 | tf_op jit(solution)/shard_map/all_to_all | solution.py:15
  66.2 0.7 broadcast_in_dim.5
  66.9 5.4 %all-to-all-start.2 = ((f32[32,1,16,128]{3,2,1,0:T(8,128)}), f32[32,1,16,128]{3,2,1,0:T(8,128)S(1)}, u32[]{:S(2)}, u32[]{:S(2)}) async-start(f32[32,1,16,128]{3,2,1,0:T(8,128)} %broadcast_in_dim.5), calls=%async_computation.2 | async-start | bytes 524288 | tf_op jit(solution)/shard_map/all_to_all | solution.py:15
  72.4 0.0 collective-permute-done.2
  72.4 0.1 select_bitcast_fusion.1
  72.4 0.1 broadcast_select_fusion.7
  72.5 0.1 broadcast_select_fusion.6
  72.7 0.2 reshape.61
  72.9 10.3 %all-to-all-done.2 = f32[32,1,16,128]{3,2,1,0:T(8,128)S(1)} async-done(((f32[32,1,16,128]{3,2,1,0:T(8,128)}), f32[32,1,16,128]{3,2,1,0:T(8,128)S(1)}, u32[]{:S(2)}, u32[]{:S(2)}) %all-to-all-start.2) | async-done | bytes 262176 | tf_op jit(solution)/shard_map/all_to_all | solution.py:15
  83.2 0.5 convolution_bitcast_fusion
  83.7 0.1 copy.44
  83.8 0.6 convolution_bitcast_fusion.1
  84.4 0.8 copy.45
  85.2 7.4 %all-to-all-start.3 = ((f32[8,3,32,128]{3,2,1,0:T(8,128)}), f32[8,3,32,128]{3,2,1,0:T(8,128)S(1)}, u32[]{:S(2)}, u32[]{:S(2)}) async-start(f32[8,3,32,128]{3,2,1,0:T(8,128)} %bitcast.26), calls=%async_computation.3 | async-start | bytes 786432 | tf_op jit(solution)/shard_map/all_to_all | solution.py:15
  92.6 0.0 copy-done
  92.6 0.1 constant_dynamic-slice_fusion.1
  92.7 0.8 constant_dynamic-slice_fusion
  93.5 7.1 %all-to-all-done.3 = f32[8,3,32,128]{3,2,1,0:T(8,128)S(1)} async-done(((f32[8,3,32,128]{3,2,1,0:T(8,128)}), f32[8,3,32,128]{3,2,1,0:T(8,128)S(1)}, u32[]{:S(2)}, u32[]{:S(2)}) %all-to-all-start.3) | async-done | bytes 393248 | tf_op jit(solution)/shard_map/all_to_all | solution.py:15
  100.6 0.7 bitcast_add_fusion
  (18 shorter events, 0.3 us)
Async XLA Ops:
  0.0 92.6 %copy-start = (f32[3,512]{1,0:T(4,128)S(1)}, f32[3,512]{1,0:T(4,128)}, u32[]{:S(2)}) copy-start(f32[3,512]{1,0:T(4,128)} %param.7) | copy-start | bytes 18436
  0.0 1.1 %copy-start.1 = (f32[512,128]{1,0:T(8,128)S(1)}, f32[512,128]{1,0:T(8,128)}, u32[]{:S(2)}) copy-start(f32[512,128]{1,0:T(8,128)} %slab_ref.1) | copy-start | bytes 786436
  1.2 7.7 %collective-permute-start = (f32[352,128]{1,0:T(8,128)S(1)}, f32[352,128]{1,0:T(8,128)S(1)}, u32[]{:S(2)}, u32[]{:S(2)}) collective-permute-start(f32[352,128]{1,0:T(8,128)S(1)} %pad_maximum_fusion.10), channel_id=1, source_target_pairs={{0,1},{1,0},{2,3},{3,2},{4,5},{5,4},{6,7},{7,6},{8,9},{9,8},{10,11... | collective-permute-start | bytes 540680 | tf_op jit(solution)/shard_map/ppermute | solution.py:25
  8.9 13.0 %collective-permute-start.1 = (f32[448,128]{1,0:T(8,128)S(1)}, f32[448,128]{1,0:T(8,128)S(1)}, u32[]{:S(2)}, u32[]{:S(2)}) collective-permute-start(f32[448,128]{1,0:T(8,128)S(1)} %pad_maximum_fusion.9), channel_id=1, source_target_pairs={{0,2},{1,3},{2,0},{3,1},{4,6},{5,7},{6,4},{7,5},{8,10},{9,11},{10,... | collective-permute-start | bytes 688136 | tf_op jit(solution)/shard_map/ppermute | solution.py:25
  22.0 50.3 %collective-permute-start.2 = (f32[4,224,128]{2,1,0:T(8,128)S(1)}, f32[4,224,128]{2,1,0:T(8,128)S(1)}, u32[]{:S(2)}, u32[]{:S(2)}) collective-permute-start(f32[4,224,128]{2,1,0:T(8,128)S(1)} %pad_maximum_fusion.5), channel_id=1, source_target_pairs={{0,16},{16,0},{1,17},{17,1},{2,18},{18,2},{3,19},{19,3},{4,20},{20... | collective-permute-start | bytes 1376264 | tf_op jit(solution)/shard_map/ppermute | solution.py:25
  48.4 17.8 %all-to-all-start.1 = ((f32[3,16,128]{2,1,0:T(8,128)}), f32[3,16,128]{2,1,0:T(8,128)S(1)}, u32[]{:S(2)}, u32[]{:S(2)}) async-start(f32[3,16,128]{2,1,0:T(8,128)} %broadcast_in_dim.4), calls=%async_computation.1 | async-start | bytes 49152 | tf_op jit(solution)/shard_map/all_to_all | solution.py:15
  66.9 16.3 %all-to-all-start.2 = ((f32[32,1,16,128]{3,2,1,0:T(8,128)}), f32[32,1,16,128]{3,2,1,0:T(8,128)S(1)}, u32[]{:S(2)}, u32[]{:S(2)}) async-start(f32[32,1,16,128]{3,2,1,0:T(8,128)} %broadcast_in_dim.5), calls=%async_computation.2 | async-start | bytes 524288 | tf_op jit(solution)/shard_map/all_to_all | solution.py:15
  85.2 15.3 %all-to-all-start.3 = ((f32[8,3,32,128]{3,2,1,0:T(8,128)}), f32[8,3,32,128]{3,2,1,0:T(8,128)S(1)}, u32[]{:S(2)}, u32[]{:S(2)}) async-start(f32[8,3,32,128]{3,2,1,0:T(8,128)} %bitcast.26), calls=%async_computation.3 | async-start | bytes 786432 | tf_op jit(solution)/shard_map/all_to_all | solution.py:15

commit v2 on v1

--- a/solution.py
+++ b/solution.py
@@ -68,14 +68,14 @@
         rowset, jnp.bitwise_xor(me, j), 1 if GATHER == "zl" else 0, keepdims=False
     ).reshape(n_slab, width)
     ops = lax.dynamic_index_in_dim(sphere_ops.reshape(nc, n_ops, width), core, 0, keepdims=False)
-    near = jnp.concatenate([pick(1), ops, pick(3)], axis=0)
+    sent_a = jnp.concatenate([pick(2), ops, pick(3)], axis=0)
     own = jnp.concatenate([pick(0), ops], axis=0)
-    to_far = pick(2)
-    got_near = swap(near, GATHER, 1)
-    far = jnp.concatenate([to_far, ops, got_near[n_slab + n_ops :], got_near[n_slab : n_slab + n_ops]], axis=0)
-    got_far = swap(far, GATHER, 2)
+    beside = pick(1)
+    got_a = swap(sent_a, GATHER, 2)
+    sent_b = jnp.concatenate([beside, ops, got_a[n_slab + n_ops :], got_a[n_slab : n_slab + n_ops]], axis=0)
+    got_b = swap(sent_b, GATHER, 1)
     n_all = n_slab + n_ops
-    stacked = jnp.stack([own, got_near[:n_all], got_far[:n_all], got_far[n_all:]])
+    stacked = jnp.stack([own, got_b[:n_all], got_a[:n_all], got_b[n_all:]])
     other = swap(stacked, "c", 1)
     both = [jnp.where(core == c, stacked, other) for c in range(nc)]
     got = jnp.stack(both, axis=1)

time: 102 us -> 102 us (level)
  starting transfers between devices: 46.3 us -> 42.9 us
  waiting for transfers between devices: 32.7 us -> 35.3 us
    ppermute x3, starting transfers between devices: 22.3 us -> 17.3 us  [swap(): return lax.ppermute(block, axis, [(i, i ^ bit) for i in range(n)])]
    ppermute x3, waiting for transfers between devices: 8.69 us -> 11.3 us  [swap(): return lax.ppermute(block, axis, [(i, i ^ bit) for i in range(n)])]
    all_to_all x3, starting transfers between devices: 24 us -> 25.6 us  [exchange(): return lax.all_to_all(blocks, axes, 0, 0, tiled=True)]
where the time goes in v2:
time: 102 us; the launch traced here: 101 us
  starting transfers between devices  42.9 us (42%)
  waiting for transfers between devices  35.3 us (35%)
  blocking collectives  14 us (14%)
  local copies, waits for them, and re-layouts  4.4 us (4%)
  Pallas kernels  2.11 us (2%)
  other arithmetic  1.13 us (1%)
  matrix products  1.05 us (1%)
    all_to_all x3, starting transfers between devices, exchange(): return lax.all_to_all(blocks, axes, 0, 0, tiled=True)  25.6 us
    all_to_all x3, waiting for transfers between devices, exchange(): return lax.all_to_all(blocks, axes, 0, 0, tiled=True)  24 us
    ppermute x3, starting transfers between devices, swap(): return lax.ppermute(block, axis, [(i, i ^ bit) for i in range(n)])  17.3 us
    all_to_all x1, blocking collectives, exchange(): return lax.all_to_all(blocks, axes, 0, 0, tiled=True)  14 us
    ppermute x3, waiting for transfers between devices, swap(): return lax.ppermute(block, axis, [(i, i ^ bit) for i in range(n)])  11.3 us
    pallas_call x1, Pallas kernels, apply(): pl.pallas_call(first_kernel, out_shape=f32(ny * nc, sub, half), in_specs=...  2.11 us
  transfers between devices with their start and end apart: 6, of which 5 were waited for; matrix products, arithmetic and copies ran while one was open for 3% of the time, Pallas kernels for 2%

profile of v2, /device:TPU:1, one launch (start us, length us, event | category | flops | bytes accessed | tf_op | source)
XLA Modules:
  0.0 101.2 jit_solution(14916735634265072481)
XLA Ops:
  0.0 0.0 copy-start
  0.0 0.0 copy-start.1
  0.0 1.1 %reshape.57 = f32[2,96,128]{2,1,0:T(8,128)S(1)} reshape(f32[3,2,64,64]{3,2,1,0:T(8,128)} %param.6) | data formatting | bytes 196608 | tf_op jit(solution)/shard_map/reshape | solution.py:70
  1.1 0.0 copy-done.1
  1.2 6.6 %collective-permute-start = (f32[352,128]{1,0:T(8,128)S(1)}, f32[352,128]{1,0:T(8,128)S(1)}, u32[]{:S(2)}, u32[]{:S(2)}) collective-permute-start(f32[352,128]{1,0:T(8,128)S(1)} %pad_maximum_fusion.10), channel_id=1, source_target_pairs={{0,2},{1,3},{2,0},{3,1},{4,6},{5,7},{6,4},{7,5},{8,10},{9,11},{10,... | collective-permute-start | bytes 540680 | tf_op jit(solution)/shard_map/ppermute | solution.py:25
  7.8 6.7 %collective-permute-done = f32[352,128]{1,0:T(8,128)S(1)} collective-permute-done((f32[352,128]{1,0:T(8,128)S(1)}, f32[352,128]{1,0:T(8,128)S(1)}, u32[]{:S(2)}, u32[]{:S(2)}) %collective-permute-start) | collective-permute-done | bytes 180256 | tf_op jit(solution)/shard_map/ppermute | solution.py:25
  14.6 2.5 %collective-permute-start.1 = (f32[448,128]{1,0:T(8,128)S(1)}, f32[448,128]{1,0:T(8,128)S(1)}, u32[]{:S(2)}, u32[]{:S(2)}) collective-permute-start(f32[448,128]{1,0:T(8,128)S(1)} %pad_maximum_fusion.9), channel_id=1, source_target_pairs={{0,1},{1,0},{2,3},{3,2},{4,5},{5,4},{6,7},{7,6},{8,9},{9,8},{10,11... | collective-permute-start | bytes 688136 | tf_op jit(solution)/shard_map/ppermute | solution.py:25
  17.1 4.6 %collective-permute-done.1 = f32[448,128]{1,0:T(8,128)S(1)} collective-permute-done((f32[448,128]{1,0:T(8,128)S(1)}, f32[448,128]{1,0:T(8,128)S(1)}, u32[]{:S(2)}, u32[]{:S(2)}) %collective-permute-start.1) | collective-permute-done | bytes 229408 | tf_op jit(solution)/shard_map/ppermute | solution.py:25
  21.8 8.1 %collective-permute-start.2 = (f32[4,224,128]{2,1,0:T(8,128)S(1)}, f32[4,224,128]{2,1,0:T(8,128)S(1)}, u32[]{:S(2)}, u32[]{:S(2)}) collective-permute-start(f32[4,224,128]{2,1,0:T(8,128)S(1)} %pad_maximum_fusion.5), channel_id=1, source_target_pairs={{0,16},{16,0},{1,17},{17,1},{2,18},{18,2},{3,19},{19,3},{4,20},{20... | collective-permute-start | bytes 1376264 | tf_op jit(solution)/shard_map/ppermute | solution.py:25
  29.9 2.1 %first_dot.1 = f32[16,16,128]{2,1,0:T(8,128)} custom-call(f32[512,128]{1,0:T(8,128)} %slab_ref.1, f32[512,256]{1,0:T(8,128)} %orb_ref.1), custom_call_target="tpu_custom_call" | custom-call | tf_op jit(solution)/shard_map/first_dot/pallas_call | solution.py:60
  32.0 14.0 %all_to_all.20 = f32[16,16,128]{2,1,0:T(8,128)S(1)} all-to-all(f32[16,16,128]{2,1,0:T(8,128)} %first_dot.1), channel_id=1, replica_groups=mesh['y'=8,'zh'=3,'c'=2,'x'=4,'zl'=4] {'y','c'}, dimensions={0} | all-to-all | bytes 262144 | tf_op jit(solution)/shard_map/all_to_all | solution.py:15
  46.1 0.6 broadcast_in_dim.4
  46.7 11.9 %all-to-all-start.1 = ((f32[3,16,128]{2,1,0:T(8,128)}), f32[3,16,128]{2,1,0:T(8,128)S(1)}, u32[]{:S(2)}, u32[]{:S(2)}) async-start(f32[3,16,128]{2,1,0:T(8,128)} %broadcast_in_dim.4), calls=%async_computation.1 | async-start | bytes 49152 | tf_op jit(solution)/shard_map/all_to_all | solution.py:15
  58.6 6.6 %all-to-all-done.1 = f32[3,16,128]{2,1,0:T(8,128)S(1)} async-done(((f32[3,16,128]{2,1,0:T(8,128)}), f32[3,16,128]{2,1,0:T(8,128)S(1)}, u32[]{:S(2)}, u32[]{:S(2)}) %all-to-all-start.1) | async-done | bytes 24608 | tf_op jit(solution)/shard_map/all_to_all | solution.py:15
  65.2 0.7 broadcast_in_dim.5
  66.0 6.2 %all-to-all-start.2 = ((f32[32,1,16,128]{3,2,1,0:T(8,128)}), f32[32,1,16,128]{3,2,1,0:T(8,128)S(1)}, u32[]{:S(2)}, u32[]{:S(2)}) async-start(f32[32,1,16,128]{3,2,1,0:T(8,128)} %broadcast_in_dim.5), calls=%async_computation.2 | async-start | bytes 524288 | tf_op jit(solution)/shard_map/all_to_all | solution.py:15
  72.2 0.0 collective-permute-done.2
  72.2 0.1 select_bitcast_fusion.1
  72.3 0.1 broadcast_select_fusion.7
  72.4 0.1 broadcast_select_fusion.6
  72.5 0.2 reshape.61
  72.7 10.3 %all-to-all-done.2 = f32[32,1,16,128]{3,2,1,0:T(8,128)S(1)} async-done(((f32[32,1,16,128]{3,2,1,0:T(8,128)}), f32[32,1,16,128]{3,2,1,0:T(8,128)S(1)}, u32[]{:S(2)}, u32[]{:S(2)}) %all-to-all-start.2) | async-done | bytes 262176 | tf_op jit(solution)/shard_map/all_to_all | solution.py:15
  83.1 0.4 convolution_bitcast_fusion
  83.5 0.1 copy.44
  83.6 0.6 convolution_bitcast_fusion.1
  84.3 0.8 copy.45
  85.0 7.5 %all-to-all-start.3 = ((f32[8,3,32,128]{3,2,1,0:T(8,128)}), f32[8,3,32,128]{3,2,1,0:T(8,128)S(1)}, u32[]{:S(2)}, u32[]{:S(2)}) async-start(f32[8,3,32,128]{3,2,1,0:T(8,128)} %bitcast.26), calls=%async_computation.3 | async-start | bytes 786432 | tf_op jit(solution)/shard_map/all_to_all | solution.py:15
  92.5 0.0 copy-done
  92.5 0.1 constant_dynamic-slice_fusion.1
  92.6 0.8 constant_dynamic-slice_fusion
  93.4 7.1 %all-to-all-done.3 = f32[8,3,32,128]{3,2,1,0:T(8,128)S(1)} async-done(((f32[8,3,32,128]{3,2,1,0:T(8,128)}), f32[8,3,32,128]{3,2,1,0:T(8,128)S(1)}, u32[]{:S(2)}, u32[]{:S(2)}) %all-to-all-start.3) | async-done | bytes 393248 | tf_op jit(solution)/shard_map/all_to_all | solution.py:15
  100.5 0.7 bitcast_add_fusion
  (18 shorter events, 0.3 us)
Async XLA Ops:
  0.0 92.5 %copy-start = (f32[3,512]{1,0:T(4,128)S(1)}, f32[3,512]{1,0:T(4,128)}, u32[]{:S(2)}) copy-start(f32[3,512]{1,0:T(4,128)} %param.7) | copy-start | bytes 18436
  0.0 1.1 %copy-start.1 = (f32[512,128]{1,0:T(8,128)S(1)}, f32[512,128]{1,0:T(8,128)}, u32[]{:S(2)}) copy-start(f32[512,128]{1,0:T(8,128)} %slab_ref.1) | copy-start | bytes 786436
  1.2 13.4 %collective-permute-start = (f32[352,128]{1,0:T(8,128)S(1)}, f32[352,128]{1,0:T(8,128)S(1)}, u32[]{:S(2)}, u32[]{:S(2)}) collective-permute-start(f32[352,128]{1,0:T(8,128)S(1)} %pad_maximum_fusion.10), channel_id=1, source_target_pairs={{0,2},{1,3},{2,0},{3,1},{4,6},{5,7},{6,4},{7,5},{8,10},{9,11},{10,... | collective-permute-start | bytes 540680 | tf_op jit(solution)/shard_map/ppermute | solution.py:25
  14.6 7.1 %collective-permute-start.1 = (f32[448,128]{1,0:T(8,128)S(1)}, f32[448,128]{1,0:T(8,128)S(1)}, u32[]{:S(2)}, u32[]{:S(2)}) collective-permute-start(f32[448,128]{1,0:T(8,128)S(1)} %pad_maximum_fusion.9), channel_id=1, source_target_pairs={{0,1},{1,0},{2,3},{3,2},{4,5},{5,4},{6,7},{7,6},{8,9},{9,8},{10,11... | collective-permute-start | bytes 688136 | tf_op jit(solution)/shard_map/ppermute | solution.py:25
  21.8 50.4 %collective-permute-start.2 = (f32[4,224,128]{2,1,0:T(8,128)S(1)}, f32[4,224,128]{2,1,0:T(8,128)S(1)}, u32[]{:S(2)}, u32[]{:S(2)}) collective-permute-start(f32[4,224,128]{2,1,0:T(8,128)S(1)} %pad_maximum_fusion.5), channel_id=1, source_target_pairs={{0,16},{16,0},{1,17},{17,1},{2,18},{18,2},{3,19},{19,3},{4,20},{20... | collective-permute-start | bytes 1376264 | tf_op jit(solution)/shard_map/ppermute | solution.py:25
  46.7 18.6 %all-to-all-start.1 = ((f32[3,16,128]{2,1,0:T(8,128)}), f32[3,16,128]{2,1,0:T(8,128)S(1)}, u32[]{:S(2)}, u32[]{:S(2)}) async-start(f32[3,16,128]{2,1,0:T(8,128)} %broadcast_in_dim.4), calls=%async_computation.1 | async-start | bytes 49152 | tf_op jit(solution)/shard_map/all_to_all | solution.py:15
  66.0 17.1 %all-to-all-start.2 = ((f32[32,1,16,128]{3,2,1,0:T(8,128)}), f32[32,1,16,128]{3,2,1,0:T(8,128)S(1)}, u32[]{:S(2)}, u32[]{:S(2)}) async-start(f32[32,1,16,128]{3,2,1,0:T(8,128)} %broadcast_in_dim.5), calls=%async_computation.2 | async-start | bytes 524288 | tf_op jit(solution)/shard_map/all_to_all | solution.py:15
  85.0 15.4 %all-to-all-start.3 = ((f32[8,3,32,128]{3,2,1,0:T(8,128)}), f32[8,3,32,128]{3,2,1,0:T(8,128)S(1)}, u32[]{:S(2)}, u32[]{:S(2)}) async-start(f32[8,3,32,128]{3,2,1,0:T(8,128)} %bitcast.26), calls=%async_computation.3 | async-start | bytes 786432 | tf_op jit(solution)/shard_map/all_to_all | solution.py:15

commit v3 on v2

v3 whole, which is shorter than its diff:
```python
import jax
import jax.numpy as jnp
from jax import lax
from jax.experimental import pallas as pl
from jax.experimental.pallas import tpu as pltpu
from jax.sharding import Mesh, PartitionSpec as P


GATHER, REDUCE = "zm", ("x", "zk")
FOURTH = (GATHER, "y")
VMEM = pl.BlockSpec(memory_space=pltpu.VMEM)


def exchange(blocks, axes):
    return lax.all_to_all(blocks, axes, 0, 0, tiled=True)


def gather(block, axes):
    n = lax.axis_size(axes)
    return exchange(jnp.broadcast_to(block[None], (n,) + block.shape), axes)


def swap(block, axis, bit):
    n = lax.axis_size(axis)
    return lax.ppermute(block, axis, [(i, i ^ bit) for i in range(n)])


def split(a):
    high = a.astype(jnp.bfloat16)
    return high, (a - high.astype(jnp.float32)).astype(jnp.bfloat16)


def dot3(a, b, dims=(((1,), (0,)), ((), ()))):
    (ah, al), (bh, bl) = a, b
    f = lambda u, v: lax.dot_general(u, v, dims, preferred_element_type=jnp.float32)
    return f(ah, bh) + (f(ah, bl) + f(al, bh))


def first_kernel(slab_ref, orb_ref, out_ref):
    n, sub, half = out_ref.shape
    nc = orb_ref.shape[1] // half
    part = dot3(split(slab_ref[...].T), split(orb_ref[...]))
    for y in range(n // nc):
        for c in range(nc):
            out_ref[c * (n // nc) + y] = part[y * sub : (y + 1) * sub, c * half : (c + 1) * half]


def apply(slab, orbitals, sphere_ops, wave_terms):
    ny, _, nc, nx, nzk = (lax.axis_size(n) for n in ("y", "zh", "c", "x", "zk"))
    ng, nr = lax.axis_size(GATHER), nx * nzk
    rows, width = slab.shape
    nb = orbitals.shape[1]
    half = nb // nc
    own_rows = rows // (ng * nr)
    nd, atoms, lm = sphere_ops.shape[:3]
    sub = width // ny
    me, core = lax.axis_index(GATHER), lax.axis_index("c")
    f32 = lambda *s: jax.ShapeDtypeStruct(s, jnp.float32)

    part = pl.pallas_call(
        first_kernel, out_shape=f32(ny * nc, sub, half), in_specs=[VMEM] * 2, out_specs=VMEM, name="first_dot"
    )(slab, orbitals)
    mine = exchange(part, ("c", "y"))

    n_slab, n_ops = nr * own_rows, nd * lm // nc
    rowset = slab.reshape(nx, ng, nzk, own_rows, width)
    pick = lambda g: lax.dynamic_index_in_dim(rowset, g, 1, keepdims=False).reshape(n_slab, width)
    ops = lax.dynamic_index_in_dim(sphere_ops.reshape(nc, n_ops, width), core, 0, keepdims=False)
    sent = jnp.concatenate([pick(1 - me), ops], axis=0)
    own = jnp.concatenate([pick(me), ops], axis=0)
    moved = swap(sent, GATHER, 1)
    stacked = jnp.stack([own, moved])
    other = swap(stacked, "c", 1)
    both = [jnp.where(core == c, stacked, other) for c in range(nc)]
    got = jnp.stack(both, axis=1)
    got = jnp.stack([jnp.where(me == 0, got[0], got[1]), jnp.where(me == 0, got[1], got[0])])
    slab_g = got[:, :, :n_slab]
    ops_g = got[:, :, n_slab:].reshape(ng, nd, atoms, lm, lm)

    first_row = lax.axis_index(("x", "zm", "zk")) * own_rows
    own_orbitals = lax.dynamic_slice_in_dim(orbitals, first_row, own_rows, 0)
    own_factors = lax.dynamic_slice_in_dim(wave_terms, first_row, own_rows, 1)
    local = own_factors[:, :, None] * own_orbitals[None]

    mine = mine.sum(0)
    mine = lax.psum(mine, "zh")
    coeffs = gather(mine, FOURTH).reshape(ng, ny, sub, half)
    coeffs = coeffs.reshape(ng, atoms, lm, half)
    inner = jnp.einsum("gdalm,gamb->dgalb", ops_g, coeffs, precision=lax.Precision.HIGH)
    inner = inner.reshape(nd, ng, width, half)
    terms = jnp.einsum("gcws,dgsb->cdwb", slab_g, inner, precision=lax.Precision.HIGH)
    terms = terms.reshape(nc, nd, nr, own_rows, half).transpose(0, 2, 1, 3, 4)
    summed = exchange(terms.reshape(nc * nr, nd, own_rows, half), ("c",) + REDUCE)
    summed = summed.reshape(nc, nr, nd, own_rows, half).sum(1)
    summed = summed.transpose(1, 2, 0, 3).reshape(nd, own_rows, nb)
    return summed + local


def solution(mesh):
    fine = Mesh(mesh.devices.reshape(8, 3, 2, 4, 2, 2), ("y", "zh", "c", "x", "zm", "zk"))
    wave, atom = ("y", "zh", "c"), ("x", "zm", "zk")
    return jax.shard_map(
        apply,
        mesh=fine,
        in_specs=(P(wave, atom), P(wave, None), P(None, atom, None, None), P(None, wave)),
        out_specs=P(None, wave + atom, None),
        check_vma=False,
    )
```

time: 102 us -> 90.5 us (0.89)
  starting transfers between devices: 42.9 us -> 32.2 us
  blocking collectives: 14 us -> 15.9 us
  waiting for transfers between devices: 35.3 us -> 33.5 us
    psum x0 -> x1, blocking collectives: none -> 15.9 us  [apply(): mine = lax.psum(mine, 'zh')]
    all_to_all x1 -> x0, blocking collectives: 14 us -> none  [exchange(): return lax.all_to_all(blocks, axes, 0, 0, tiled=True)]
    all_to_all x3, starting transfers between devices: 25.6 us -> 18.3 us  [exchange(): return lax.all_to_all(blocks, axes, 0, 0, tiled=True)]
    ppermute x3 -> x2, waiting for transfers between devices: 11.3 us -> 6.73 us  [swap(): return lax.ppermute(block, axis, [(i, i ^ bit) for i in range(n)])]
    ppermute x3 -> x2, starting transfers between devices: 17.3 us -> 13.9 us  [swap(): return lax.ppermute(block, axis, [(i, i ^ bit) for i in range(n)])]
    all_to_all x3, waiting for transfers between devices: 24 us -> 26.7 us  [exchange(): return lax.all_to_all(blocks, axes, 0, 0, tiled=True)]
    transpose x1 -> x2, local copies, waits for them, and re-layouts: 0.02 us -> 1.21 us  [the longest x1 0.95 us: apply(): terms = terms.reshape(nc, nd, nr, own_rows, half).transpose(0, 2, 1, 3, 4)]
  transfers between devices with their start and end apart: 6 -> 5, of which waited for: 5 -> 4; matrix products, arithmetic and copies ran while one was open for 3% -> 2% of each run, Pallas kernels for 2% -> 2%
where the time goes in v3:
time: 90.5 us; the launch traced here: 90 us
  waiting for transfers between devices  33.5 us (37%)
  starting transfers between devices  32.2 us (36%)
  blocking collectives  15.9 us (18%)
  local copies, waits for them, and re-layouts  3.98 us (4%)
  Pallas kernels  2.1 us (2%)
  matrix products  1.16 us (1%)
  other arithmetic  0.97 us (1%)
    all_to_all x3, waiting for transfers between devices, exchange(): return lax.all_to_all(blocks, axes, 0, 0, tiled=True)  26.7 us
    all_to_all x3, starting transfers between devices, exchange(): return lax.all_to_all(blocks, axes, 0, 0, tiled=True)  18.3 us
    psum x1, blocking collectives, apply(): mine = lax.psum(mine, 'zh')  15.9 us
    ppermute x2, starting transfers between devices, swap(): return lax.ppermute(block, axis, [(i, i ^ bit) for i in range(n)])  13.9 us
    ppermute x2, waiting for transfers between devices, swap(): return lax.ppermute(block, axis, [(i, i ^ bit) for i in range(n)])  6.73 us
    pallas_call x1, Pallas kernels, apply(): pl.pallas_call(first_kernel, out_shape=f32(ny * nc, sub, half), in_specs=...  2.1 us
  transfers between devices with their start and end apart: 5, of which 4 were waited for; matrix products, arithmetic and copies ran while one was open for 2% of the time, Pallas kernels for 2%

profile of v3, /device:TPU:1, one launch (start us, length us, event | category | flops | bytes accessed | tf_op | source)
XLA Modules:
  0.0 90.0 jit_solution(8016603600988885279)
XLA Ops:
  0.0 0.0 copy-start
  0.0 0.0 copy-start.1
  0.0 1.1 %reshape.37 = f32[2,96,128]{2,1,0:T(8,128)S(1)} reshape(f32[3,2,64,64]{3,2,1,0:T(8,128)} %param.6) | data formatting | bytes 196608 | tf_op jit(solution)/shard_map/reshape | solution.py:68
  1.1 0.0 copy-done.1
  1.2 6.6 %collective-permute-start = (f32[352,128]{1,0:T(8,128)S(1)}, f32[352,128]{1,0:T(8,128)S(1)}, u32[]{:S(2)}, u32[]{:S(2)}) collective-permute-start(f32[352,128]{1,0:T(8,128)S(1)} %get-tuple-element.12), channel_id=1, source_target_pairs={{0,2},{2,0},{1,3},{3,1},{4,6},{6,4},{5,7},{7,5},{8,10},{10,8},{9,1... | collective-permute-start | bytes 540680 | tf_op jit(solution)/shard_map/ppermute | solution.py:25
  7.8 6.7 %collective-permute-done = f32[352,128]{1,0:T(8,128)S(1)} collective-permute-done((f32[352,128]{1,0:T(8,128)S(1)}, f32[352,128]{1,0:T(8,128)S(1)}, u32[]{:S(2)}, u32[]{:S(2)}) %collective-permute-start) | collective-permute-done | bytes 180256 | tf_op jit(solution)/shard_map/ppermute | solution.py:25
  14.6 7.3 %collective-permute-start.1 = (f32[2,352,128]{2,1,0:T(8,128)S(1)}, f32[2,352,128]{2,1,0:T(8,128)S(1)}, u32[]{:S(2)}, u32[]{:S(2)}) collective-permute-start(f32[2,352,128]{2,1,0:T(8,128)S(1)} %pad_maximum_fusion.2), channel_id=1, source_target_pairs={{0,16},{16,0},{1,17},{17,1},{2,18},{18,2},{3,19},{19,3},{4,20},{20... | collective-permute-start | bytes 1081352 | tf_op jit(solution)/shard_map/ppermute | solution.py:25
  21.9 2.1 %first_dot.1 = f32[16,16,128]{2,1,0:T(8,128)} custom-call(f32[512,128]{1,0:T(8,128)} %slab_ref.1, f32[512,256]{1,0:T(8,128)} %orb_ref.1), custom_call_target="tpu_custom_call" | custom-call | tf_op jit(solution)/shard_map/first_dot/pallas_call | solution.py:60
  24.0 4.5 %all-to-all-start = ((f32[16,16,128]{2,1,0:T(8,128)}), f32[16,16,128]{2,1,0:T(8,128)S(1)}, u32[]{:S(2)}, u32[]{:S(2)}) async-start(f32[16,16,128]{2,1,0:T(8,128)} %first_dot.1), calls=%async_computation | async-start | bytes 262144 | tf_op jit(solution)/shard_map/all_to_all | solution.py:15
  28.4 7.4 %all-to-all-done = f32[16,16,128]{2,1,0:T(8,128)S(1)} async-done(((f32[16,16,128]{2,1,0:T(8,128)}), f32[16,16,128]{2,1,0:T(8,128)S(1)}, u32[]{:S(2)}, u32[]{:S(2)}) %all-to-all-start) | async-done | bytes 131104 | tf_op jit(solution)/shard_map/all_to_all | solution.py:15
  35.8 15.9 %psum.7 = f32[16,128]{1,0:T(8,128)S(1)} all-reduce(f32[16,128]{1,0:T(8,128)S(1)} %reduce_sum.18), channel_id=1, replica_groups=mesh['y'=8,'zh'=3,'c'=2,'x'=4,'zm'=2,'zk'=2] {'zh'}, use_global_device_ids=true, to_apply=%region_1.2 | all-reduce | flops 2048 | bytes 16384 | tf_op jit(solution)/shard_map/psum | solution.py:86
  51.8 0.7 broadcast_in_dim.2
  52.4 3.5 %all-to-all-start.1 = ((f32[16,16,128]{2,1,0:T(8,128)}), f32[16,16,128]{2,1,0:T(8,128)S(1)}, u32[]{:S(2)}, u32[]{:S(2)}) async-start(f32[16,16,128]{2,1,0:T(8,128)} %broadcast_in_dim.2), calls=%async_computation.1 | async-start | bytes 262144 | tf_op jit(solution)/shard_map/all_to_all | solution.py:15
  56.0 0.0 collective-permute-done.1
  56.0 0.1 select_bitcast_fusion.1
  56.0 0.1 broadcast_select_fusion.1
  56.1 0.1 reshape.39
  56.3 8.0 %all-to-all-done.1 = f32[16,16,128]{2,1,0:T(8,128)S(1)} async-done(((f32[16,16,128]{2,1,0:T(8,128)}), f32[16,16,128]{2,1,0:T(8,128)S(1)}, u32[]{:S(2)}, u32[]{:S(2)}) %all-to-all-start.1) | async-done | bytes 131104 | tf_op jit(solution)/shard_map/all_to_all | solution.py:15
  64.3 0.3 convolution_bitcast_fusion.1
  64.6 0.9 convolution_bitcast_fusion
  65.5 0.3 copy.29
  65.8 1.0 %copy.30 = f32[2,8,3,32,128]{4,3,2,1,0:T(8,128)} copy(f32[2,8,3,32,128]{4,3,1,2,0:T(8,128)S(1)} %bitcast.54) | data formatting | bytes 1572864 | tf_op jit(solution)/shard_map/transpose | solution.py:92
  66.7 10.3 %all-to-all-start.2 = ((f32[16,3,32,128]{3,2,1,0:T(8,128)}), f32[16,3,32,128]{3,2,1,0:T(8,128)S(1)}, u32[]{:S(2)}, u32[]{:S(2)}) async-start(f32[16,3,32,128]{3,2,1,0:T(8,128)} %bitcast.20), calls=%async_computation.2 | async-start | bytes 1572864 | tf_op jit(solution)/shard_map/all_to_all | solution.py:15
  77.0 0.0 copy-done
  77.0 0.1 constant_dynamic-slice_fusion.1
  77.1 0.8 constant_dynamic-slice_fusion
  77.8 11.4 %all-to-all-done.2 = f32[16,3,32,128]{3,2,1,0:T(8,128)S(1)} async-done(((f32[16,3,32,128]{3,2,1,0:T(8,128)}), f32[16,3,32,128]{3,2,1,0:T(8,128)S(1)}, u32[]{:S(2)}, u32[]{:S(2)}) %all-to-all-start.2) | async-done | bytes 786464 | tf_op jit(solution)/shard_map/all_to_all | solution.py:15
  89.2 0.1 bitcast_reduce_fusion
  89.2 0.7 bitcast_add_fusion
  (8 shorter events, 0.2 us)
Async XLA Ops:
  0.0 77.0 %copy-start = (f32[3,512]{1,0:T(4,128)S(1)}, f32[3,512]{1,0:T(4,128)}, u32[]{:S(2)}) copy-start(f32[3,512]{1,0:T(4,128)} %param.7) | copy-start | bytes 18436
  0.0 1.1 %copy-start.1 = (f32[512,128]{1,0:T(8,128)S(1)}, f32[512,128]{1,0:T(8,128)}, u32[]{:S(2)}) copy-start(f32[512,128]{1,0:T(8,128)} %slab_ref.1) | copy-start | bytes 786436
  1.2 13.4 %collective-permute-start = (f32[352,128]{1,0:T(8,128)S(1)}, f32[352,128]{1,0:T(8,128)S(1)}, u32[]{:S(2)}, u32[]{:S(2)}) collective-permute-start(f32[352,128]{1,0:T(8,128)S(1)} %get-tuple-element.12), channel_id=1, source_target_pairs={{0,2},{2,0},{1,3},{3,1},{4,6},{6,4},{5,7},{7,5},{8,10},{10,8},{9,1... | collective-permute-start | bytes 540680 | tf_op jit(solution)/shard_map/ppermute | solution.py:25
  14.6 41.4 %collective-permute-start.1 = (f32[2,352,128]{2,1,0:T(8,128)S(1)}, f32[2,352,128]{2,1,0:T(8,128)S(1)}, u32[]{:S(2)}, u32[]{:S(2)}) collective-permute-start(f32[2,352,128]{2,1,0:T(8,128)S(1)} %pad_maximum_fusion.2), channel_id=1, source_target_pairs={{0,16},{16,0},{1,17},{17,1},{2,18},{18,2},{3,19},{19,3},{4,20},{20... | collective-permute-start | bytes 1081352 | tf_op jit(solution)/shard_map/ppermute | solution.py:25
  24.0 11.8 %all-to-all-start = ((f32[16,16,128]{2,1,0:T(8,128)}), f32[16,16,128]{2,1,0:T(8,128)S(1)}, u32[]{:S(2)}, u32[]{:S(2)}) async-start(f32[16,16,128]{2,1,0:T(8,128)} %first_dot.1), calls=%async_computation | async-start | bytes 262144 | tf_op jit(solution)/shard_map/all_to_all | solution.py:15
  52.4 11.9 %all-to-all-start.1 = ((f32[16,16,128]{2,1,0:T(8,128)}), f32[16,16,128]{2,1,0:T(8,128)S(1)}, u32[]{:S(2)}, u32[]{:S(2)}) async-start(f32[16,16,128]{2,1,0:T(8,128)} %broadcast_in_dim.2), calls=%async_computation.1 | async-start | bytes 262144 | tf_op jit(solution)/shard_map/all_to_all | solution.py:15
  66.7 22.5 %all-to-all-start.2 = ((f32[16,3,32,128]{3,2,1,0:T(8,128)}), f32[16,3,32,128]{3,2,1,0:T(8,128)S(1)}, u32[]{:S(2)}, u32[]{:S(2)}) async-start(f32[16,3,32,128]{3,2,1,0:T(8,128)} %bitcast.20), calls=%async_computation.2 | async-start | bytes 1572864 | tf_op jit(solution)/shard_map/all_to_all | solution.py:15

commit v4 on v2

--- a/solution.py
+++ b/solution.py
@@ -7,7 +7,7 @@
 
 
 GATHER, REDUCE = "zl", "x"
-THIRD, FOURTH = ("zh",), ("y", GATHER)
+THIRD, FOURTH = ("zh",), (GATHER, "y")
 VMEM = pl.BlockSpec(memory_space=pltpu.VMEM)
 
 
@@ -39,10 +39,10 @@
 def first_kernel(slab_ref, orb_ref, out_ref):
     n, sub, half = out_ref.shape
     nc = orb_ref.shape[1] // half
-    part = dot3(split(slab_ref[...].T), split(orb_ref[...]))
+    part = dot3(split(slab_ref[...]), split(orb_ref[...]), (((0,), (0,)), ((), ())))
     for y in range(n // nc):
         for c in range(nc):
-            out_ref[y * nc + c] = part[y * sub : (y + 1) * sub, c * half : (c + 1) * half]
+            out_ref[c * (n // nc) + y] = part[y * sub : (y + 1) * sub, c * half : (c + 1) * half]
 
 
 def apply(slab, orbitals, sphere_ops, wave_terms):
@@ -60,7 +60,7 @@
     part = pl.pallas_call(
         first_kernel, out_shape=f32(ny * nc, sub, half), in_specs=[VMEM] * 2, out_specs=VMEM, name="first_dot"
     )(slab, orbitals)
-    mine = exchange(part, ("y", "c"))
+    mine = exchange(part, ("c", "y"))
 
     n_slab, n_ops = nr * own_rows, nd * lm // nc
     rowset = slab.reshape(nx, nzl, own_rows, width)
@@ -93,8 +93,8 @@
     mine = mine.sum(0)
     mine = gather(mine, THIRD).reshape((nzh, -1, sub, half))
     mine = mine.sum(0)
-    coeffs = gather(mine, FOURTH).reshape(ny, ng, sub, half)
-    coeffs = coeffs.transpose(1, 0, 2, 3).reshape(ng, atoms, lm, half)
+    coeffs = gather(mine, FOURTH).reshape(ng, ny, sub, half)
+    coeffs = coeffs.reshape(ng, atoms, lm, half)
     inner = jnp.einsum("gdalm,gamb->dgalb", ops_g, coeffs, precision=lax.Precision.HIGH)
     inner = inner.reshape(nd, ng, width, half)
     terms = jnp.einsum("gcws,dgsb->cdwb", slab_g, inner, precision=lax.Precision.HIGH)

time: 102 us -> 101 us (level)
  blocking collectives: 14 us -> 12.5 us
  starting transfers between devices: 42.9 us -> 44.3 us
    all_to_all x1, blocking collectives: 14 us -> 12.5 us  [exchange(): return lax.all_to_all(blocks, axes, 0, 0, tiled=True)]
    all_to_all x3, starting transfers between devices: 25.6 us -> 27 us  [exchange(): return lax.all_to_all(blocks, axes, 0, 0, tiled=True)]
where the time goes in v4:
time: 101 us; the launch traced here: 100 us
  starting transfers between devices  44.3 us (44%)
  waiting for transfers between devices  34.8 us (34%)
  blocking collectives  12.5 us (12%)
  local copies, waits for them, and re-layouts  4.38 us (4%)
  Pallas kernels  2.1 us (2%)
  other arithmetic  1.13 us (1%)
  matrix products  1.05 us (1%)
    all_to_all x3, starting transfers between devices, exchange(): return lax.all_to_all(blocks, axes, 0, 0, tiled=True)  27 us
    all_to_all x3, waiting for transfers between devices, exchange(): return lax.all_to_all(blocks, axes, 0, 0, tiled=True)  23.5 us
    ppermute x3, starting transfers between devices, swap(): return lax.ppermute(block, axis, [(i, i ^ bit) for i in range(n)])  17.3 us
    all_to_all x1, blocking collectives, exchange(): return lax.all_to_all(blocks, axes, 0, 0, tiled=True)  12.5 us
    ppermute x3, waiting for transfers between devices, swap(): return lax.ppermute(block, axis, [(i, i ^ bit) for i in range(n)])  11.3 us
    pallas_call x1, Pallas kernels, apply(): pl.pallas_call(first_kernel, out_shape=f32(ny * nc, sub, half), in_specs=...  2.1 us
  transfers between devices with their start and end apart: 6, of which 5 were waited for; matrix products, arithmetic and copies ran while one was open for 3% of the time, Pallas kernels for 2%

profile of v4, /device:TPU:1, one launch (start us, length us, event | category | flops | bytes accessed | tf_op | source)
XLA Modules:
  0.0 100.5 jit_solution(4503796207409725206)
XLA Ops:
  0.0 0.0 copy-start
  0.0 0.0 copy-start.1
  0.0 1.1 %reshape.49 = f32[2,96,128]{2,1,0:T(8,128)S(1)} reshape(f32[3,2,64,64]{3,2,1,0:T(8,128)} %param.6) | data formatting | bytes 196608 | tf_op jit(solution)/shard_map/reshape | solution.py:70
  1.1 0.0 copy-done.1
  1.2 6.6 %collective-permute-start = (f32[352,128]{1,0:T(8,128)S(1)}, f32[352,128]{1,0:T(8,128)S(1)}, u32[]{:S(2)}, u32[]{:S(2)}) collective-permute-start(f32[352,128]{1,0:T(8,128)S(1)} %pad_maximum_fusion.10), channel_id=1, source_target_pairs={{0,2},{1,3},{2,0},{3,1},{4,6},{5,7},{6,4},{7,5},{8,10},{9,11},{10,... | collective-permute-start | bytes 540680 | tf_op jit(solution)/shard_map/ppermute | solution.py:25
  7.8 6.7 %collective-permute-done = f32[352,128]{1,0:T(8,128)S(1)} collective-permute-done((f32[352,128]{1,0:T(8,128)S(1)}, f32[352,128]{1,0:T(8,128)S(1)}, u32[]{:S(2)}, u32[]{:S(2)}) %collective-permute-start) | collective-permute-done | bytes 180256 | tf_op jit(solution)/shard_map/ppermute | solution.py:25
  14.6 2.5 %collective-permute-start.1 = (f32[448,128]{1,0:T(8,128)S(1)}, f32[448,128]{1,0:T(8,128)S(1)}, u32[]{:S(2)}, u32[]{:S(2)}) collective-permute-start(f32[448,128]{1,0:T(8,128)S(1)} %pad_maximum_fusion.9), channel_id=1, source_target_pairs={{0,1},{1,0},{2,3},{3,2},{4,5},{5,4},{6,7},{7,6},{8,9},{9,8},{10,11... | collective-permute-start | bytes 688136 | tf_op jit(solution)/shard_map/ppermute | solution.py:25
  17.1 4.6 %collective-permute-done.1 = f32[448,128]{1,0:T(8,128)S(1)} collective-permute-done((f32[448,128]{1,0:T(8,128)S(1)}, f32[448,128]{1,0:T(8,128)S(1)}, u32[]{:S(2)}, u32[]{:S(2)}) %collective-permute-start.1) | collective-permute-done | bytes 229408 | tf_op jit(solution)/shard_map/ppermute | solution.py:25
  21.8 8.1 %collective-permute-start.2 = (f32[4,224,128]{2,1,0:T(8,128)S(1)}, f32[4,224,128]{2,1,0:T(8,128)S(1)}, u32[]{:S(2)}, u32[]{:S(2)}) collective-permute-start(f32[4,224,128]{2,1,0:T(8,128)S(1)} %pad_maximum_fusion.5), channel_id=1, source_target_pairs={{0,16},{16,0},{1,17},{17,1},{2,18},{18,2},{3,19},{19,3},{4,20},{20... | collective-permute-start | bytes 1376264 | tf_op jit(solution)/shard_map/ppermute | solution.py:25
  29.9 2.1 %first_dot.1 = f32[16,16,128]{2,1,0:T(8,128)} custom-call(f32[512,128]{1,0:T(8,128)} %slab_ref.1, f32[512,256]{1,0:T(8,128)} %orb_ref.1), custom_call_target="tpu_custom_call" | custom-call | tf_op jit(solution)/shard_map/first_dot/pallas_call | solution.py:60
  32.0 12.5 %all_to_all.20 = f32[16,16,128]{2,1,0:T(8,128)S(1)} all-to-all(f32[16,16,128]{2,1,0:T(8,128)} %first_dot.1), channel_id=1, replica_groups=mesh['y'=8,'zh'=3,'c'=2,'x'=4,'zl'=4] {'c','y'}, dimensions={0} | all-to-all | bytes 262144 | tf_op jit(solution)/shard_map/all_to_all | solution.py:15
  44.6 0.6 broadcast_in_dim.4
  45.2 11.9 %all-to-all-start.1 = ((f32[3,16,128]{2,1,0:T(8,128)}), f32[3,16,128]{2,1,0:T(8,128)S(1)}, u32[]{:S(2)}, u32[]{:S(2)}) async-start(f32[3,16,128]{2,1,0:T(8,128)} %broadcast_in_dim.4), calls=%async_computation.1 | async-start | bytes 49152 | tf_op jit(solution)/shard_map/all_to_all | solution.py:15
  57.1 6.6 %all-to-all-done.1 = f32[3,16,128]{2,1,0:T(8,128)S(1)} async-done(((f32[3,16,128]{2,1,0:T(8,128)}), f32[3,16,128]{2,1,0:T(8,128)S(1)}, u32[]{:S(2)}, u32[]{:S(2)}) %all-to-all-start.1) | async-done | bytes 24608 | tf_op jit(solution)/shard_map/all_to_all | solution.py:15
  63.7 0.7 broadcast_in_dim.5
  64.4 7.5 %all-to-all-start.2 = ((f32[32,1,16,128]{3,2,1,0:T(8,128)}), f32[32,1,16,128]{3,2,1,0:T(8,128)S(1)}, u32[]{:S(2)}, u32[]{:S(2)}) async-start(f32[32,1,16,128]{3,2,1,0:T(8,128)} %broadcast_in_dim.5), calls=%async_computation.2 | async-start | bytes 524288 | tf_op jit(solution)/shard_map/all_to_all | solution.py:15
  71.9 0.0 collective-permute-done.2
  71.9 0.1 select_bitcast_fusion.1
  72.0 0.1 broadcast_select_fusion.7
  72.1 0.1 broadcast_select_fusion.6
  72.2 0.2 reshape.53
  72.4 9.8 %all-to-all-done.2 = f32[32,1,16,128]{3,2,1,0:T(8,128)S(1)} async-done(((f32[32,1,16,128]{3,2,1,0:T(8,128)}), f32[32,1,16,128]{3,2,1,0:T(8,128)S(1)}, u32[]{:S(2)}, u32[]{:S(2)}) %all-to-all-start.2) | async-done | bytes 262176 | tf_op jit(solution)/shard_map/all_to_all | solution.py:15
  82.2 0.5 convolution_bitcast_fusion
  82.6 0.1 copy.40
  82.7 0.6 convolution_bitcast_fusion.1
  83.4 0.8 copy.41
  84.2 7.6 %all-to-all-start.3 = ((f32[8,3,32,128]{3,2,1,0:T(8,128)}), f32[8,3,32,128]{3,2,1,0:T(8,128)S(1)}, u32[]{:S(2)}, u32[]{:S(2)}) async-start(f32[8,3,32,128]{3,2,1,0:T(8,128)} %bitcast.24), calls=%async_computation.3 | async-start | bytes 786432 | tf_op jit(solution)/shard_map/all_to_all | solution.py:15
  91.8 0.0 copy-done
  91.8 0.1 constant_dynamic-slice_fusion.1
  91.9 0.8 constant_dynamic-slice_fusion
  92.6 7.1 %all-to-all-done.3 = f32[8,3,32,128]{3,2,1,0:T(8,128)S(1)} async-done(((f32[8,3,32,128]{3,2,1,0:T(8,128)}), f32[8,3,32,128]{3,2,1,0:T(8,128)S(1)}, u32[]{:S(2)}, u32[]{:S(2)}) %all-to-all-start.3) | async-done | bytes 393248 | tf_op jit(solution)/shard_map/all_to_all | solution.py:15
  99.8 0.7 bitcast_add_fusion
  (17 shorter events, 0.3 us)
Async XLA Ops:
  0.0 91.8 %copy-start = (f32[3,512]{1,0:T(4,128)S(1)}, f32[3,512]{1,0:T(4,128)}, u32[]{:S(2)}) copy-start(f32[3,512]{1,0:T(4,128)} %param.7) | copy-start | bytes 18436
  0.0 1.1 %copy-start.1 = (f32[512,128]{1,0:T(8,128)S(1)}, f32[512,128]{1,0:T(8,128)}, u32[]{:S(2)}) copy-start(f32[512,128]{1,0:T(8,128)} %slab_ref.1) | copy-start | bytes 786436
  1.2 13.4 %collective-permute-start = (f32[352,128]{1,0:T(8,128)S(1)}, f32[352,128]{1,0:T(8,128)S(1)}, u32[]{:S(2)}, u32[]{:S(2)}) collective-permute-start(f32[352,128]{1,0:T(8,128)S(1)} %pad_maximum_fusion.10), channel_id=1, source_target_pairs={{0,2},{1,3},{2,0},{3,1},{4,6},{5,7},{6,4},{7,5},{8,10},{9,11},{10,... | collective-permute-start | bytes 540680 | tf_op jit(solution)/shard_map/ppermute | solution.py:25
  14.6 7.1 %collective-permute-start.1 = (f32[448,128]{1,0:T(8,128)S(1)}, f32[448,128]{1,0:T(8,128)S(1)}, u32[]{:S(2)}, u32[]{:S(2)}) collective-permute-start(f32[448,128]{1,0:T(8,128)S(1)} %pad_maximum_fusion.9), channel_id=1, source_target_pairs={{0,1},{1,0},{2,3},{3,2},{4,5},{5,4},{6,7},{7,6},{8,9},{9,8},{10,11... | collective-permute-start | bytes 688136 | tf_op jit(solution)/shard_map/ppermute | solution.py:25
  21.8 50.1 %collective-permute-start.2 = (f32[4,224,128]{2,1,0:T(8,128)S(1)}, f32[4,224,128]{2,1,0:T(8,128)S(1)}, u32[]{:S(2)}, u32[]{:S(2)}) collective-permute-start(f32[4,224,128]{2,1,0:T(8,128)S(1)} %pad_maximum_fusion.5), channel_id=1, source_target_pairs={{0,16},{16,0},{1,17},{17,1},{2,18},{18,2},{3,19},{19,3},{4,20},{20... | collective-permute-start | bytes 1376264 | tf_op jit(solution)/shard_map/ppermute | solution.py:25
  45.2 18.6 %all-to-all-start.1 = ((f32[3,16,128]{2,1,0:T(8,128)}), f32[3,16,128]{2,1,0:T(8,128)S(1)}, u32[]{:S(2)}, u32[]{:S(2)}) async-start(f32[3,16,128]{2,1,0:T(8,128)} %broadcast_in_dim.4), calls=%async_computation.1 | async-start | bytes 49152 | tf_op jit(solution)/shard_map/all_to_all | solution.py:15
  64.4 17.7 %all-to-all-start.2 = ((f32[32,1,16,128]{3,2,1,0:T(8,128)}), f32[32,1,16,128]{3,2,1,0:T(8,128)S(1)}, u32[]{:S(2)}, u32[]{:S(2)}) async-start(f32[32,1,16,128]{3,2,1,0:T(8,128)} %broadcast_in_dim.5), calls=%async_computation.2 | async-start | bytes 524288 | tf_op jit(solution)/shard_map/all_to_all | solution.py:15
  84.2 15.5 %all-to-all-start.3 = ((f32[8,3,32,128]{3,2,1,0:T(8,128)}), f32[8,3,32,128]{3,2,1,0:T(8,128)S(1)}, u32[]{:S(2)}, u32[]{:S(2)}) async-start(f32[8,3,32,128]{3,2,1,0:T(8,128)} %bitcast.24), calls=%async_computation.3 | async-start | bytes 786432 | tf_op jit(solution)/shard_map/all_to_all | solution.py:15
